TPU v7x, 256 devices: a whole 4x4x8 slice. The times are simulated.
256 devices in a mesh: tm: 64 (over z_hi, y, x), freq: 4 (over z_lo, core).
Axes of the slice: x: 4, y: 4, z: 8 (z_hi: 4, z_lo: 2; z = z_hi * 2 + z_lo), core: 2. Of those that a mesh axis runs over, the one named last changes fastest.
Arguments:
- spectrum: bfloat16 [1024, 49152], P('freq', 'tm'), may hold values from 0.0099487305 to 10
- decay_rate: float32 [1024], P('freq'), may hold values from 1e-07 to 0.03
- init_state: float32 [1024], P('freq'), may hold values from 0.3 to 3
- clip_ids: int32 [49152], P('tm'), may hold values from 0 to 5, never falling along the last dimension, each value on 1 to 16384 neighbouring positions
- encoder: bfloat16 [256, 1024], P(None, 'freq'), may hold values from -0.1875 to 0.1875
- gauss_noise: float32 [256, 49152], P(None, 'tm'), may hold values from -3 to 3
- uniform_noise: float32 [2, 256, 49152], P(None, None, 'tm'), may hold values from 0.02 to 1
- boost_count: int32 [256], replicated, may hold values from 1 to 2
- templates: bfloat16 [1024, 4096], P('freq'), may hold values from 0.0099487305 to 1
Outputs:
- frame_loss: float32 [49152], P('tm')
- template_grad: float32 [4096, 1024], P('tm', 'freq')
Inputs may be any that keep to these rules, and one draw needn't show every extreme that they name: `clip_ids`: clip numbers never fall along the frames; each clip holds 1 to 16384 frames, one exactly that many.
All inputs are finite; a program needn't handle non-finite values.
Results may differ from a plain program's by a relative error of at most 0.00033.
Values may be sent and summed in bfloat16 or wider, within the bound.
A program may use at most 64 MiB of HBM per device.

v0:
```python
import jax
import jax.numpy as jnp
from jax import lax
from jax.sharding import PartitionSpec as P

F = 1024
K = 256
L = 16


def prefix(part, axis, combine, identity):
    place = lax.axis_index(axis)
    gathered = jax.tree.map(lambda a: lax.all_gather(a, axis), part)
    state = jax.tree.map(lambda a, e: jnp.zeros_like(a) + jnp.asarray(e, a.dtype), part, identity)

    def one(lap, state):
        return combine(
            state, jax.tree.map(lambda a: lax.dynamic_index_in_dim(a, lap, 0, False), gathered)
        )

    return lax.fori_loop(0, place, one, state)


def passed_along(value, axis, steps):
    count = lax.axis_size(axis)
    leading, last = (max(0, -steps), min(count, count - steps))
    return lax.ppermute(value, axis, [(source, source + steps) for source in range(leading, last)])


def compose(former, latter):
    return (former[0] * latter[0], latter[0] * former[1] + latter[1])


def linked(former, latter):
    p_one, q_one, first_one, last_one, start_one, mark_one = former
    p_two, q_two, first_two, last_two, start_two, mark_two = latter
    joined = (last_one >= 0.0) & (first_two >= 0.0) & (first_two != last_one)
    factor = jnp.where(joined, 0.8, 1.0)
    scaled = p_two * factor
    merged_p = scaled * p_one
    merged_q = scaled * q_one + q_two
    first_clip = jnp.where(first_one >= 0.0, first_one, first_two)
    start_frame = jnp.where(first_one >= 0.0, start_one, start_two)
    last_clip = jnp.where(last_two >= 0.0, last_two, last_one)
    latest = jnp.maximum(jnp.maximum(mark_one, jnp.where(joined, start_two, -1.0)), mark_two)
    return (merged_p, merged_q, first_clip, last_clip, start_frame, latest)


def topic_mixture(logits, gaussian, uniforms, boost_count):
    concentration = jax.nn.softplus(logits) + 0.5
    boosted = boost_count[:, None]
    shape_total = concentration + boosted.astype(jnp.float32)
    offset = shape_total - 1.0 / 3.0
    spread = lax.rsqrt(9.0 * offset)
    linear = 1.0 + spread * gaussian
    gamma_draw = offset * linear * linear * linear * jnp.exp(jnp.log(uniforms[0]) / concentration)
    gamma_draw = gamma_draw * jnp.where(
        boosted >= 2, jnp.exp(jnp.log(uniforms[1]) / (concentration + 1.0)), 1.0
    )
    return (gamma_draw / jnp.sum(gamma_draw, axis=0, keepdims=True)).astype(jnp.bfloat16)


def on_device(
    spectrum,
    decay_rate,
    init_state,
    clip_ids,
    encoder,
    gauss_noise,
    uniform_noise,
    boost_count,
    templates,
):
    frames = spectrum.shape[1]
    bins = spectrum.shape[0]
    rim_width = L - 1
    spectral = spectrum.astype(jnp.float32)
    changed = clip_ids[1:] != clip_ids[:-1]
    factor_row = jnp.concatenate(
        [jnp.ones((1,), jnp.float32), jnp.where(changed, 0.8, 1.0).astype(jnp.float32)]
    )
    rates = (1.0 - decay_rate)[:, None] * factor_row[None, :]
    inputs = decay_rate[:, None] * spectral
    running, summed = lax.associative_scan(compose, (rates, inputs), axis=1)
    anchor = lax.axis_index("tm") * frames
    positions = anchor + jnp.arange(frames, dtype=jnp.int32)
    marks = jnp.where(jnp.concatenate([jnp.zeros((1,), bool), changed]), positions, -1)
    clip_float = clip_ids.astype(jnp.float32)
    summary = (
        running[:, -1],
        summed[:, -1],
        clip_float[:1],
        clip_float[-1:],
        jnp.reshape(anchor.astype(jnp.float32), (1,)),
        jnp.reshape(jnp.max(marks).astype(jnp.float32), (1,)),
    )
    minus_one = jnp.full((1,), -1.0, jnp.float32)
    identity_tuple = (
        jnp.ones((bins,), jnp.float32),
        jnp.zeros((bins,), jnp.float32),
        minus_one,
        minus_one,
        minus_one,
        minus_one,
    )
    before = prefix(summary, "tm", linked, identity_tuple)
    junction = (before[3] >= 0.0) & (clip_float[:1] != before[3])
    entry = jnp.where(junction, 0.8, 1.0) * (before[0] * init_state + before[1])
    smooth = running * entry[:, None] + summed
    normed = (spectral * lax.rsqrt(smooth + 0.1)).astype(jnp.bfloat16)
    code_part = jnp.dot(encoder, normed, preferred_element_type=jnp.float32)
    logits = lax.psum(code_part, "freq")
    proportions = topic_mixture(logits, gauss_noise, uniform_noise, boost_count)
    topics = proportions.shape[0]
    rim = passed_along(proportions[:, frames - rim_width :], "tm", 1)
    extended = jnp.concatenate([rim, proportions], axis=1)
    flags = jnp.concatenate([junction, changed]).astype(jnp.int32)
    clean = jnp.cumsum(flags) == 0
    clip_pad = jnp.concatenate([jnp.full((rim_width,), -1, jnp.int32), clip_ids])
    lag_rows = []
    mask_rows = []
    for lag in range(L):
        begin = rim_width - lag
        lag_rows.append(extended[:, begin : begin + frames])
        source = jnp.arange(frames, dtype=jnp.int32) - lag
        same_clip = clip_pad[begin : begin + frames] == clip_ids
        earlier = clean & (before[5] <= (anchor + source).astype(jnp.float32))
        mask_rows.append(jnp.where(source >= 0, same_clip, earlier))
    valid = jnp.stack(mask_rows).astype(jnp.bfloat16)
    stacked = (jnp.stack(lag_rows, axis=1) * valid[None]).reshape(topics * L, frames)
    recon = jnp.dot(templates, stacked, preferred_element_type=jnp.float32)
    sums_part = (
        jnp.sum(recon, axis=0),
        jnp.sum(spectral, axis=0),
        jnp.sum(spectral * jnp.log(recon), axis=0),
    )
    recon_sum, spec_sum, log_sum = lax.psum((sums_part[0], sums_part[1], sums_part[2]), "freq")
    frame_loss = jnp.log(recon_sum) - log_sum / spec_sum
    scale_factor = F * K / (frames * lax.axis_size("tm"))
    ratio = (
        scale_factor * (1.0 / recon_sum[None, :] - spectral / (spec_sum[None, :] * recon))
    ).astype(jnp.bfloat16)
    owned_rows = topics * L // lax.axis_size("tm")
    full_grad = lax.dot_general(
        stacked, ratio, (((1,), (1,)), ((), ())), preferred_element_type=jnp.float32
    )
    total_grad = lax.psum(full_grad, "tm")
    template_grad = lax.dynamic_slice_in_dim(
        total_grad, lax.axis_index("tm") * owned_rows, owned_rows, 0
    )
    return (frame_loss, template_grad)


def solution(mesh):
    placed = (
        P("freq", "tm"),
        P("freq"),
        P("freq"),
        P("tm"),
        P(None, "freq"),
        P(None, "tm"),
        P(None, None, "tm"),
        P(),
        P("freq", None),
    )
    return jax.shard_map(
        on_device, mesh=mesh, in_specs=placed, out_specs=(P("tm"), P("tm", "freq")), check_vma=False
    )
```

profile of v0, /device:TPU:2, one launch (start us, length us, event | category | flops | bytes accessed | tf_op | source)
XLA Modules:
  0.0 1997.8 jit_solution(15807336264710183670)
XLA Ops:
  17.0 3.1 slice.440
  20.2 3.2 slice.439
  23.3 2.3 fusion.127
  98.1 3.2 slice.480
  121.8 2.5 pad.144
  133.7 2.9 pad.128
  137.3 187.8 %all-gather = f32[16384,1]{0,1:T(1,128)S(1)} all-gather(f32[256,1]{0,1:T(1,128)S(1)} %slice_add_fusion.3), channel_id=2, replica_groups=mesh['tm'=64,'freq'=4] {'tm'}, dimensions={0}, use_global_device_ids=true | all-gather | bytes 66560 | tf_op jit(solution)/shard_map/all_gather | solution.py:13
  335.1 2.9 pad.145
  337.9 2.8 pad.146
  341.5 191.4 %all-gather.2 = f32[16384,1]{0,1:T(1,128)S(1)} all-gather(f32[256,1]{0,1:T(1,128)S(1)} %slice_add_fusion), channel_id=4, replica_groups=mesh['tm'=64,'freq'=4] {'tm'}, dimensions={0}, use_global_device_ids=true | all-gather | bytes 66560 | tf_op jit(solution)/shard_map/all_gather | solution.py:13
  535.8 186.1 %all-reduce.41 = (f32[64]{0:T(128)S(1)}, f32[64]{0:T(128)S(1)}, f32[64]{0:T(128)S(1)}, f32[64]{0:T(128)S(1)}) all-reduce(f32[64]{0:T(128)S(1)} %get-tuple-element.234, f32[64]{0:T(128)} %copy-done.6, f32[64]{0:T(128)S(1)} %dynamic-update-slice.2, f32[64]{0:T(128)S(1)} %dynamic-update-slice.3), channel_id=3, replica_groups=mesh['tm'=64,'freq'=4] {'tm'}, use_global_device_ids=true, to_apply=%add.37 | all-reduce | flops 256 | bytes 2048
  722.0 6.6 while.20
  729.9 3.0 convolution_bitcast_fusion
  733.0 2.3 fusion.126
  735.3 2.3 copy.87
  740.8 435.0 %all-reduce.46.cloned.1.call-done = f32[256,768]{0,1:T(8,128)} async-done(((f32[256,768]{0,1:T(8,128)}), f32[256,768]{0,1:T(8,128)}) %all-reduce.46.cloned.1.call-update) | async-done | bytes 786448 | tf_op jit(solution)/shard_map/psum | solution.py:112
  1175.8 2.8 fusion.124
  1179.5 3.5 collective-permute-start
  1197.7 7.2 broadcast_multiply_fusion
  1204.9 9.0 copy.83
  1213.9 5.5 fusion.136
  1221.1 10.1 all-reduce.42
  1231.9 6.8 fusion.11
  1238.7 750.8 %all-reduce.48.cloned.1.call-done = f32[4096,256]{1,0:T(8,128)} async-done(((f32[4096,256]{1,0:T(8,128)}), f32[4096,256]{1,0:T(8,128)}) %all-reduce.48.cloned.1.call-update) | async-done | bytes 4194320 | tf_op jit(solution)/shard_map/psum | solution.py:147
  (242 shorter events, 151.2 us)
Async XLA Ops:
  7.2 1206.8 %copy-start = (bf16[256,4096]{1,0:T(8,128)(2,1)S(1)}, bf16[256,4096]{1,0:T(8,128)(2,1)}, u32[]{:S(2)}) copy-start(bf16[256,4096]{1,0:T(8,128)(2,1)} %param.19) | copy-start | bytes 6291460
  7.2 1168.6 %all-reduce.46.cloned.1.call-start = ((), (), s32[]{:S(2)}) async-start(), calls=%async_computation | async-start | bytes 1572864 | tf_op jit(solution)/shard_map/psum | solution.py:112
  9.6 92.4 %copy-start.1 = (f32[256,768]{0,1:T(8,128)}, f32[256,768]{0,1:T(8,128)S(1)}, u32[]{:S(2)}) copy-start(f32[256,768]{0,1:T(8,128)S(1)} %broadcast_multiply_fusion.1) | copy-start | bytes 2359300
  15.4 86.6 %copy-start.3 = (s32[768]{0:T(1024)S(1)}, s32[768]{0:T(1024)}, u32[]{:S(2)}) copy-start(s32[768]{0:T(1024)} %param.14) | copy-start | bytes 9220
  113.3 18.5 slice-start
  119.8 212.0 %copy-start.4 = (pred[767]{0:T(1024)(128)(4,1)S(1)}, pred[767]{0:T(1024)(128)(4,1)}, u32[]{:S(2)}) copy-start(pred[767]{0:T(1024)(128)(4,1)} %get-tuple-element.180) | copy-start | bytes 2305
  119.8 213.5 %slice-start.1 = ((f32[256,768]{0,1:T(8,128)}), f32[256,1]{0,1:T(1,128)S(1)}, s32[]{:S(2)}) async-start(f32[256,768]{0,1:T(8,128)} %convert_multiply_fusion.2), calls=%async_computation.3 | async-start | bytes 2048 | tf_op jit(solution)/shard_map/slice | solution.py:84
  128.7 601.2 %copy-start.2 = (bf16[256,256]{1,0:T(8,128)(2,1)S(1)}, bf16[256,256]{1,0:T(8,128)(2,1)}, u32[]{:S(2)}) copy-start(bf16[256,256]{1,0:T(8,128)(2,1)} %param.15) | copy-start | bytes 393220
  331.8 9.0 copy-start.6
  729.9 10.2 copy-start.5
  732.9 1256.6 %all-reduce.48.cloned.1.call-start = ((), (), s32[]{:S(2)}) async-start(), calls=%async_computation.1 | async-start | bytes 8388608 | tf_op jit(solution)/shard_map/psum | solution.py:147
  1179.5 5.5 collective-permute-start
Sparse Core Ops, SparseCore 0:
  733.0 442.7 all-reduce.45
  1238.8 750.6 all-reduce.47
where the time goes:
time: 2010 us; the launch traced here: 2000 us
  waiting for transfers between devices  1190 us (59%)
  blocking collectives  575 us (29%)
  local copies, waits for them, and re-layouts  126 us (6%)
  other arithmetic  70.4 us (4%)
    psum x1, waiting for transfers between devices, on_device(): total_grad = lax.psum(full_grad, 'tm')  751 us
    psum x1, waiting for transfers between devices, on_device(): logits = lax.psum(code_part, 'freq')  435 us
    all_gather x2, blocking collectives, prefix(): gathered = jax.tree.map(lambda a: lax.all_gather(a, axis), part)  379 us
    unnamed x1, blocking collectives  186 us
    slice x66, local copies, waits for them, and re-layouts, on_device(): running, summed = lax.associative_scan(compose, (rates, inputs), axis=1)  77.9 us
  transfers between devices with their start and end apart: 3, of which 3 were waited for; matrix products, arithmetic and copies ran while one was open for 0% of the time, Pallas kernels for 0%

commit v1 on v0

--- a/solution.py
+++ b/solution.py
@@ -109,7 +109,7 @@
     smooth = running * entry[:, None] + summed
     normed = (spectral * lax.rsqrt(smooth + 0.1)).astype(jnp.bfloat16)
     code_part = jnp.dot(encoder, normed, preferred_element_type=jnp.float32)
-    logits = lax.psum(code_part, "freq")
+    logits = jnp.sum(lax.all_gather(code_part, "freq"), axis=0)
     proportions = topic_mixture(logits, gauss_noise, uniform_noise, boost_count)
     topics = proportions.shape[0]
     rim = passed_along(proportions[:, frames - rim_width :], "tm", 1)

time: 2010 us -> 1920 us (0.955)
  waiting for transfers between devices: 1190 us -> 1100 us
    psum x1 -> x0, waiting for transfers between devices: 435 us -> none  [on_device(): logits = lax.psum(code_part, 'freq')]
    all_gather x0 -> x1, waiting for transfers between devices: none -> 342 us  [on_device(): logits = jnp.sum(lax.all_gather(code_part, 'freq'), axis=0)]
  transfers between devices with their start and end apart: 3 -> 3, of which waited for: 3 -> 3; matrix products, arithmetic and copies ran while one was open for 0% -> 1% of each run, Pallas kernels for 0% -> 0%
where the time goes in v1:
time: 1920 us; the launch traced here: 1910 us
  waiting for transfers between devices  1100 us (57%)
  blocking collectives  575 us (30%)
  local copies, waits for them, and re-layouts  127 us (7%)
  other arithmetic  73.5 us (4%)
    psum x1, waiting for transfers between devices, on_device(): total_grad = lax.psum(full_grad, 'tm')  751 us
    all_gather x2, blocking collectives, prefix(): gathered = jax.tree.map(lambda a: lax.all_gather(a, axis), part)  379 us
    all_gather x1, waiting for transfers between devices, on_device(): logits = jnp.sum(lax.all_gather(code_part, 'freq'), axis=0)  342 us
    unnamed x1, blocking collectives  186 us
    slice x66, local copies, waits for them, and re-layouts, on_device(): running, summed = lax.associative_scan(compose, (rates, inputs), axis=1)  71.4 us
  transfers between devices with their start and end apart: 3, of which 3 were waited for; matrix products, arithmetic and copies ran while one was open for 1% of the time, Pallas kernels for 0%

profile of v1, /device:TPU:2, one launch (start us, length us, event | category | flops | bytes accessed | tf_op | source)
XLA Modules:
  0.0 1910.1 jit_solution(15880466620702573484)
XLA Ops:
  17.0 3.2 slice.440
  20.2 3.2 slice.439
  91.5 3.2 slice.480
  117.2 2.5 pad.144
  130.3 2.9 pad.128
  133.9 187.8 %all-gather = f32[16384,1]{0,1:T(1,128)S(1)} all-gather(f32[256,1]{0,1:T(1,128)S(1)} %slice_add_fusion.3), channel_id=2, replica_groups=mesh['tm'=64,'freq'=4] {'tm'}, dimensions={0}, use_global_device_ids=true | all-gather | bytes 66560 | tf_op jit(solution)/shard_map/all_gather | solution.py:13
  330.0 2.9 pad.146
  333.6 191.4 %all-gather.2 = f32[16384,1]{0,1:T(1,128)S(1)} all-gather(f32[256,1]{0,1:T(1,128)S(1)} %slice_add_fusion), channel_id=4, replica_groups=mesh['tm'=64,'freq'=4] {'tm'}, dimensions={0}, use_global_device_ids=true | all-gather | bytes 66560 | tf_op jit(solution)/shard_map/all_gather | solution.py:13
  527.4 186.1 %all-reduce.41 = (f32[64]{0:T(128)S(1)}, f32[64]{0:T(128)S(1)}, f32[64]{0:T(128)S(1)}, f32[64]{0:T(128)S(1)}) all-reduce(f32[64]{0:T(128)S(1)} %get-tuple-element.234, f32[64]{0:T(128)S(1)} %slice_dynamic-update-slice_fusion, f32[64]{0:T(128)S(1)} %dynamic-update-slice.2, ...), channel_id=3, replica_groups=mesh['tm'=64,'freq'=4] {'tm'}, use_global_device_ids=true, to_apply=%add.37 | all-reduce | flops 256 | bytes 2048
  713.4 5.2 while.20
  719.4 3.1 convolution_bitcast_fusion
  722.8 2.6 fusion.126
  730.0 2.4 copy.93
  733.1 342.4 %all-gather.7.cloned.1.call-done = f32[1024,768]{0,1:T(8,128)} async-done(((f32[256,768]{0,1:T(8,128)}), f32[1024,768]{0,1:T(8,128)}) %all-gather.7.cloned.1.call-update) | async-done | bytes 3145744 | tf_op jit(solution)/shard_map/all_gather | solution.py:112
  1075.4 5.1 reshape.172
  1080.6 4.6 reduce_sum.45
  1085.2 3.0 fusion.124
  1089.2 3.4 collective-permute-start
  1107.3 7.3 broadcast_multiply_fusion
  1114.6 9.1 copy.98
  1123.7 5.5 fusion.136
  1132.9 10.1 all-reduce.42
  1143.6 7.0 fusion.11
  1150.6 751.2 %all-reduce.45.cloned.1.call-done = f32[4096,256]{1,0:T(8,128)} async-done(((f32[4096,256]{1,0:T(8,128)}), f32[4096,256]{1,0:T(8,128)}) %all-reduce.45.cloned.1.call-update) | async-done | bytes 4194320 | tf_op jit(solution)/shard_map/psum | solution.py:147
  (246 shorter events, 150.3 us)
Async XLA Ops:
  7.2 1116.5 %copy-start = (bf16[256,4096]{1,0:T(8,128)(2,1)S(1)}, bf16[256,4096]{1,0:T(8,128)(2,1)}, u32[]{:S(2)}) copy-start(bf16[256,4096]{1,0:T(8,128)(2,1)} %param.19) | copy-start | bytes 6291460
  7.2 1068.2 %all-gather.7.cloned.1.call-start = ((), (), s32[]{:S(2)}) async-start(), calls=%async_computation.1 | async-start | bytes 3932160 | tf_op jit(solution)/shard_map/all_gather | solution.py:112
  9.7 3.1 copy-start.1
  15.4 79.3 %copy-start.3 = (s32[768]{0:T(1024)S(1)}, s32[768]{0:T(1024)}, u32[]{:S(2)}) copy-start(s32[768]{0:T(1024)} %param.14) | copy-start | bytes 9220
  105.5 22.8 %slice-start = ((f32[256,768]{0,1:T(8,128)}), f32[256,1]{0,1:T(1,128)S(1)}, s32[]{:S(2)}) async-start(f32[256,768]{0,1:T(8,128)} %copy-done.1), calls=%async_computation.2 | async-start | bytes 2048 | tf_op jit(solution)/shard_map/slice | solution.py:84
  113.6 209.5 %copy-start.7 = (u32[256]{0:T(256)S(1)}, u32[256]{0:T(256)}, u32[]{:S(2)}) copy-start(u32[256]{0:T(256)} %constant.229) | copy-start | bytes 3076
  113.6 212.1 %copy-start.4 = (pred[767]{0:T(1024)(128)(4,1)S(1)}, pred[767]{0:T(1024)(128)(4,1)}, u32[]{:S(2)}) copy-start(pred[767]{0:T(1024)(128)(4,1)} %get-tuple-element.180) | copy-start | bytes 2305
  113.6 213.5 %slice-start.1 = ((f32[256,768]{0,1:T(8,128)}), f32[256,1]{0,1:T(1,128)S(1)}, s32[]{:S(2)}) async-start(f32[256,768]{0,1:T(8,128)} %convert_multiply_fusion.2), calls=%async_computation.3 | async-start | bytes 2048 | tf_op jit(solution)/shard_map/slice | solution.py:84
  122.2 597.1 %copy-start.6 = (f32[256]{0:T(256)S(1)}, f32[256]{0:T(256)}, u32[]{:S(2)}) copy-start(f32[256]{0:T(256)} %param.13) | copy-start | bytes 3076
  124.1 595.2 %copy-start.2 = (bf16[256,256]{1,0:T(8,128)(2,1)S(1)}, bf16[256,256]{1,0:T(8,128)(2,1)}, u32[]{:S(2)}) copy-start(bf16[256,256]{1,0:T(8,128)(2,1)} %param.15) | copy-start | bytes 393220
  719.4 13.0 copy-start.5
  722.5 1179.3 %all-reduce.45.cloned.1.call-start = ((), (), s32[]{:S(2)}) async-start(), calls=%async_computation | async-start | bytes 8388608 | tf_op jit(solution)/shard_map/psum | solution.py:147
  1089.2 5.5 collective-permute-start
Sparse Core Ops, SparseCore 0:
  722.6 352.7 all-gather.6
  1150.7 751.0 all-reduce.44
